TPU v7x, 128 devices: a whole 4x4x4 slice. The times are simulated.
128 devices in a mesh: samp: 16 (over z_hi, x, core), par: 8 (over y, z_lo).
Axes of the slice: x: 4, y: 4, z: 4 (z_hi: 2, z_lo: 2; z = z_hi * 2 + z_lo), core: 2. Of those that a mesh axis runs over, the one named last changes fastest.
Arguments:
- activations: bfloat16 [10240, 2048], P('samp', 'par'), may hold values from -128 to 128
- signal: bfloat16 [10240, 2], P('samp'), may hold values from -40 to 40
Outputs:
- gram: float32 [10240, 10240], P('samp', 'par')
- panels: float32 [10240, 1280], P('samp', 'par')
All inputs are finite; a program needn't handle non-finite values.
Results may differ from a plain program's by a relative error of at most 0.0022.
Values may be sent and summed in bfloat16 or wider, within the bound.
A program may use at most 128 MiB of HBM per device.

v0:
```python
import jax
import jax.numpy as jnp
from jax import lax
from jax.sharding import PartitionSpec as P

DAMPING = 0.5
EPSILON = 1e-05


def from_root(value, axis, root):
    mine = lax.axis_index(axis) == root
    return lax.psum(jnp.where(mine, value, jnp.zeros_like(value)), axis)


def right_solve(factor, block):
    return jax.scipy.linalg.solve_triangular(factor, block.T, lower=True).T


def first_moment(signal, active):
    return jnp.dot(signal.T, active, preferred_element_type=jnp.float32)


def second_moment(signal_float, active_float):
    products = signal_float[:, :, None] * active_float[:, None, :]
    return jnp.sum(products * products, axis=0)


def normalize(moment_one, moment_two, sample_total, slab_width):
    average = moment_one / sample_total
    column_scale = 1.0 / jnp.sqrt(
        slab_width * (moment_two / sample_total - average * average + EPSILON)
    )
    return (average, column_scale)


def build_rows(signal_float, active_float, average, column_scale):
    centered = signal_float[:, :, None] * active_float[:, None, :] - average[None]
    return (centered * column_scale[None]).astype(jnp.bfloat16)


def per_device(activations, signal):
    signal_float = signal.astype(jnp.float32)
    local_count = activations.shape[0]
    samp_count = lax.axis_size("samp")
    par_count = lax.axis_size("par")
    sample_total = local_count * samp_count
    slab_width = signal.shape[1] * activations.shape[1] * par_count
    active_float = activations.astype(jnp.float32)
    sum_one = first_moment(signal, activations)
    sum_two = second_moment(signal_float, active_float)
    moment_one, moment_two = lax.psum((sum_one, sum_two), "samp")
    average, column_scale = normalize(moment_one, moment_two, sample_total, slab_width)
    local_rows = build_rows(signal_float, active_float, average, column_scale)
    full_rows = lax.all_gather(local_rows, "par", axis=2, tiled=True).reshape(
        local_count, slab_width
    )
    blocks_per = samp_count // par_count
    column = lax.axis_index("par")
    samp_index = lax.axis_index("samp")
    pieces = []
    for offset in range(blocks_per):
        partner = from_root(full_rows, "samp", column * blocks_per + offset)
        pieces.append(
            lax.dot_general(
                full_rows, partner, (((1,), (1,)), ((), ())), preferred_element_type=jnp.float32
            )
        )
    gram_tile = jnp.concatenate(pieces, axis=1)
    global_row = samp_index * local_count + lax.broadcasted_iota(jnp.int32, gram_tile.shape, 0)
    global_col = column * (blocks_per * local_count) + lax.broadcasted_iota(
        jnp.int32, gram_tile.shape, 1
    )
    gram_tile = gram_tile + jnp.where(
        global_row == global_col, jnp.float32(DAMPING), jnp.float32(0.0)
    )
    column_block = from_root(gram_tile, "par", 0)
    identity = jnp.eye(local_count, dtype=jnp.float32)
    first_cols = column_block[:, :local_count]
    second_cols = column_block[:, local_count:]
    factor_one = jnp.linalg.cholesky(jnp.where(samp_index == 0, first_cols, identity))
    factor_one = from_root(factor_one, "samp", 0)
    panel_one = right_solve(factor_one, first_cols)
    partner_panel = from_root(panel_one, "samp", 1)
    update = second_cols - jnp.dot(panel_one, partner_panel.T, precision=lax.Precision.HIGHEST)
    factor_two = jnp.linalg.cholesky(jnp.where(samp_index == 1, update, identity))
    factor_two = from_root(factor_two, "samp", 1)
    panel_two = right_solve(factor_two, update)
    panel_two = jnp.where(samp_index == 0, jnp.float32(0.0), panel_two)
    both_panels = jnp.concatenate([panel_one, panel_two], axis=1)
    own_width = both_panels.shape[1] // par_count
    own_panels = lax.dynamic_slice_in_dim(both_panels, column * own_width, own_width, 1)
    return (gram_tile, own_panels)


def solution(mesh):
    in_specs = (P("samp", "par"), P("samp", None))
    out_specs = (P("samp", "par"), P("samp", "par"))
    return jax.shard_map(
        per_device, mesh=mesh, in_specs=in_specs, out_specs=out_specs, check_vma=False
    )
```

profile of v0, /device:TPU:1, one launch (start us, length us, event | category | flops | bytes accessed | tf_op | source)
XLA Modules:
  0.0 1360.1 jit_solution(4430709151654853441)
XLA Ops:
  10.4 34.8 %all-reduce.1 = (f32[2,256]{1,0:T(2,128)S(1)}, f32[2,256]{1,0:T(2,128)S(1)}) all-reduce(f32[2,256]{1,0:T(2,128)S(1)} %fusion.8, f32[2,256]{1,0:T(2,128)S(1)} %fusion.104), channel_id=1, replica_groups=mesh['samp'=16,'par'=8] {'samp'}, use_global_device_ids=true, to_apply=%region_2.0 | all-reduce | flops 1024 | bytes 8192 | tf_op jit(solution)/shard_map/psum | solution.py:51
  46.4 110.9 %all-gather.2.cloned.1.call-done = bf16[640,2,2048]{0,2,1:T(8,128)(2,1)} async-done(((bf16[640,2,256]{0,2,1:T(8,128)(2,1)}), bf16[640,2,2048]{0,2,1:T(8,128)(2,1)}) %all-gather.2.cloned.1.call-update) | async-done | bytes 5242896 | tf_op jit(solution)/shard_map/all_gather | solution.py:54
  157.3 7.3 broadcast_select_fusion.1
  164.7 169.7 %all-reduce.17.cloned.1.call-done = (bf16[640,4096]{0,1:T(8,128)(2,1)}, bf16[640,4096]{0,1:T(8,128)(2,1)}) async-done(((bf16[640,4096]{0,1:T(8,128)(2,1)}, bf16[640,4096]{0,1:T(8,128)(2,1)}), (bf16[640,4096]{0,1:T(8,128)(2,1)}, bf16[640,4096]{0,1:T(8,128)(2,1)})) %all-reduce.17.cloned.1.call-update) | async-done | bytes 10485776 | tf_op jit(solution)/shard_map/psum | solution.py:12
  334.4 8.6 fusion.105
  343.1 4.5 fusion.106
  347.6 3.3 broadcast_select_fusion.2
  351.0 149.1 %all-reduce.9.cloned.1.call-done = f32[640,1280]{0,1:T(8,128)} async-done(((f32[640,1280]{0,1:T(8,128)}), f32[640,1280]{0,1:T(8,128)}) %all-reduce.9.cloned.1.call-update) | async-done | bytes 3276816 | tf_op jit(solution)/shard_map/psum | solution.py:12
  500.2 2.8 convert_select_fusion.1
  503.0 1.5 copy.43
  505.8 11.7 cholesky.364
  517.7 9.8 custom-call.34
  528.9 13.2 cholesky.383
  542.1 1.5 select_reduce_fusion.8
  543.5 11.4 custom-call.35
  556.6 12.3 cholesky.404
  570.5 10.4 custom-call.36
  582.5 11.9 cholesky.423
  595.2 9.8 custom-call.37
  605.6 11.7 cholesky.440
  623.2 144.2 %all-reduce.11.cloned.1.call-done = f32[640,640]{1,0:T(8,128)} async-done(((f32[640,640]{1,0:T(8,128)}), f32[640,640]{1,0:T(8,128)}) %all-reduce.11.cloned.1.call-update) | async-done | bytes 1638416 | tf_op jit(solution)/shard_map/psum | solution.py:12
  767.5 1.5 fusion.4
  769.8 13.5 while.4
  770.8 2.0 bitcast_dynamic-update-slice_fusion.4
  773.5 2.0 bitcast_dynamic-update-slice_fusion.4
  776.1 2.0 bitcast_dynamic-update-slice_fusion.4
  778.7 2.0 bitcast_dynamic-update-slice_fusion.4
  781.3 2.0 bitcast_dynamic-update-slice_fusion.4
  783.3 50.6 %custom-call.38 = f32[5,128,128]{1,2,0:T(8,128)} custom-call(f32[5,128,128]{2,1,0:T(8,128)} %get-tuple-element.18), custom_call_target="InvertDiagBlocksLowerTriangular" | custom-call | tf_op jit(solution)/shard_map/jit(_solve_triangular)/triangular_solve | solution.py:16
  837.1 1.4 convolution_subtract_fusion.2
  839.0 1.8 convolution_subtract_fusion.5
  841.3 2.6 fusion.28
  845.5 1.5 convolution_dynamic-update-slice_fusion.1
  848.4 144.0 %all-reduce.13.cloned.1.call-done = f32[640,640]{1,0:T(8,128)} async-done(((f32[640,640]{1,0:T(8,128)}), f32[640,640]{1,0:T(8,128)}) %all-reduce.13.cloned.1.call-update) | async-done | bytes 1638416 | tf_op jit(solution)/shard_map/psum | solution.py:12
  992.4 7.7 convert_select_fusion
  1000.1 1.8 copy.52
  1001.9 1.6 fusion
  1004.7 11.7 cholesky.455
  1016.5 9.8 custom-call.39
  1029.6 13.2 cholesky.474
  1042.8 1.5 select_reduce_fusion.3
  1045.7 11.5 custom-call.40
  1058.3 1.4 convolution_subtract_fusion.8
  1059.7 12.3 cholesky.495
  1073.6 10.4 custom-call.41
  1086.5 12.1 cholesky.514
  1099.3 9.8 custom-call.42
  1110.5 11.7 cholesky.531
  1127.4 4.6 copy.59
  1132.0 139.5 %all-reduce.15.cloned.1.call-done = f32[640,640]{1,0:T(8,128)} async-done(((f32[640,640]{1,0:T(8,128)}), f32[640,640]{1,0:T(8,128)}) %all-reduce.15.cloned.1.call-update) | async-done | bytes 1638416 | tf_op jit(solution)/shard_map/psum | solution.py:12
  1271.4 1.5 fusion.2
  1273.7 13.2 while.5
  1274.4 2.0 bitcast_dynamic-update-slice_fusion.5
  1277.0 2.0 bitcast_dynamic-update-slice_fusion.5
  1279.7 2.0 bitcast_dynamic-update-slice_fusion.5
  1282.3 2.0 bitcast_dynamic-update-slice_fusion.5
  1285.0 2.0 bitcast_dynamic-update-slice_fusion.5
  1287.0 50.8 %custom-call.43 = f32[5,128,128]{1,2,0:T(8,128)} custom-call(f32[5,128,128]{2,1,0:T(8,128)} %get-tuple-element.19), custom_call_target="InvertDiagBlocksLowerTriangular" | custom-call | tf_op jit(solution)/shard_map/jit(_solve_triangular)/triangular_solve | solution.py:16
  1337.7 1.5 fusion.52
  1339.3 1.4 convolution_subtract_fusion.1
  1341.2 1.6 convolution_subtract_fusion
  1343.2 1.9 convolution_subtract_fusion.4
  1345.7 2.7 fusion.25
  1350.0 1.5 convolution_dynamic-update-slice_fusion
  (144 shorter events, 51.1 us)
Async XLA Ops:
  7.2 150.1 %all-gather.2.cloned.1.call-start = ((), (), s32[]{:S(2)}) async-start(), calls=%async_computation | async-start | bytes 5898240 | tf_op jit(solution)/shard_map/all_gather | solution.py:54
  46.4 288.1 %all-reduce.17.cloned.1.call-start = ((), (), s32[]{:S(2)}) async-start(), calls=%async_computation.5 | async-start | bytes 20971520 | tf_op jit(solution)/shard_map/psum | solution.py:12
  164.6 178.5 %slice-start = ((s8[5242880]{0:T(1024)(128)(4,1)}), s8[1048576]{0:T(1024)(128)(4,1)S(1)}, s32[]{:S(2)}) async-start(s8[5242880]{0:T(1024)(128)(4,1)} %bitcast.139), calls=%async_computation.6 | async-start | bytes 2097152
  164.6 335.5 %all-reduce.9.cloned.1.call-start = ((), (), s32[]{:S(2)}) async-start(), calls=%async_computation.1 | async-start | bytes 6553600 | tf_op jit(solution)/shard_map/psum | solution.py:12
  334.4 8.6 slice-start.1
  334.4 8.7 copy-start.10
  351.0 416.5 %all-reduce.11.cloned.1.call-start = ((), (), s32[]{:S(2)}) async-start(), calls=%async_computation.2 | async-start | bytes 3276800 | tf_op jit(solution)/shard_map/psum | solution.py:12
  504.6 1.2 copy-start.2
  505.8 21.7 %copy-start.3 = (f32[640,640]{1,0:T(8,128)S(1)}, f32[640,640]{1,0:T(8,128)}, u32[]{:S(2)}) copy-start(f32[640,640]{1,0:T(8,128)} %copy-done.2) | copy-start | bytes 4915204
  623.2 369.2 %all-reduce.13.cloned.1.call-start = ((), (), s32[]{:S(2)}) async-start(), calls=%async_computation.3 | async-start | bytes 3276800 | tf_op jit(solution)/shard_map/psum | solution.py:12
  623.2 210.7 %copy-start = (f32[640,640]{1,0:T(8,128)S(1)}, f32[640,640]{1,0:T(8,128)}, u32[]{:S(2)}) copy-start(f32[640,640]{1,0:T(8,128)} %get-tuple-element.55) | copy-start | bytes 4915204
  783.3 50.6 %copy-start.5 = (f32[640,640]{1,0:T(8,128)}, f32[640,640]{1,0:T(8,128)S(1)}, u32[]{:S(2)}) copy-start(f32[640,640]{1,0:T(8,128)S(1)} %get-tuple-element.202) | copy-start | bytes 4915204
  833.9 2.7 copy-start.8
  844.5 1.0 copy-start.6
  848.4 423.1 %all-reduce.15.cloned.1.call-start = ((), (), s32[]{:S(2)}) async-start(), calls=%async_computation.4 | async-start | bytes 3276800 | tf_op jit(solution)/shard_map/psum | solution.py:12
  1003.5 1.2 copy-start.1
  1286.9 50.8 %copy-start.4 = (f32[640,640]{1,0:T(8,128)}, f32[640,640]{1,0:T(8,128)S(1)}, u32[]{:S(2)}) copy-start(f32[640,640]{1,0:T(8,128)S(1)} %get-tuple-element.201) | copy-start | bytes 4915204
  1337.7 3.0 copy-start.9
  1349.1 1.0 copy-start.7
Sparse Core Ops, SparseCore 0:
  46.5 110.7 all-gather.1
  164.8 169.6 all-reduce.16
  351.1 149.0 all-reduce.8
  623.3 144.1 all-reduce.10
  848.5 143.8 all-reduce.12
  1127.5 143.8 all-reduce.14
where the time goes:
time: 1370 us; the launch traced here: 1360 us
  waiting for transfers between devices  858 us (63%)
  other arithmetic  342 us (25%)
  matrix products  59.1 us (4%)
  local copies, waits for them, and re-layouts  44.9 us (3%)
  blocking collectives  34.8 us (3%)
  between operations  21.2 us (2%)
    psum x5, waiting for transfers between devices, from_root(): return lax.psum(jnp.where(mine, value, jnp.zeros_like(value)), axis)  747 us
    all_gather x1, waiting for transfers between devices, per_device(): lax.all_gather(local_rows, 'par', axis=2, tiled=True)  111 us
    another operation x19, other arithmetic, per_device(): jnp.linalg.cholesky(jnp.where(samp_index == 1, update, identity))  108 us
    another operation x18, other arithmetic, per_device(): jnp.linalg.cholesky(jnp.where(samp_index == 0, first_cols, identity))  107 us
    another operation x5, other arithmetic, right_solve(): return jax.scipy.linalg.solve_triangular(factor, block.T, lower=True).T  104 us
    psum x1, blocking collectives, per_device(): moment_one, moment_two = lax.psum((sum_one, sum_two), 'samp')  34.8 us
    another operation x41, local copies, waits for them, and re-layouts, right_solve(): return jax.scipy.linalg.solve_triangular(factor, block.T, lower=True).T  29.2 us
  transfers between devices with their start and end apart: 6, of which 6 were waited for; matrix products, arithmetic and copies ran while one was open for 0% of the time, Pallas kernels for 0%

commit v1 on v0

--- a/solution.py
+++ b/solution.py
@@ -1,3 +1,4 @@
+import functools
 import jax
 import jax.numpy as jnp
 from jax import lax
@@ -5,6 +6,15 @@
 
 DAMPING = 0.5
 EPSILON = 1e-05
+
+
+def _perform_spots(u_in, bus_axis):
+    return jnp.concatenate(
+        lax.all_to_all(jnp.stack(lax.axis_size(bus_axis) * [u_in]), bus_axis, 0, 0), axis=2
+    )
+
+
+keep_up_side = functools.partial(_perform_spots, bus_axis="par")
 
 
 def from_root(value, axis, root):
@@ -51,9 +61,7 @@
     moment_one, moment_two = lax.psum((sum_one, sum_two), "samp")
     average, column_scale = normalize(moment_one, moment_two, sample_total, slab_width)
     local_rows = build_rows(signal_float, active_float, average, column_scale)
-    full_rows = lax.all_gather(local_rows, "par", axis=2, tiled=True).reshape(
-        local_count, slab_width
-    )
+    full_rows = keep_up_side(local_rows).reshape(local_count, slab_width)
     blocks_per = samp_count // par_count
     column = lax.axis_index("par")
     samp_index = lax.axis_index("samp")

time: 1370 us -> 1330 us (0.971)
  waiting for transfers between devices: 858 us -> 816 us
    all_gather x1 -> x0, waiting for transfers between devices: 111 us -> none  [per_device(): lax.all_gather(local_rows, 'par', axis=2, tiled=True)]
    all_to_all x0 -> x1, waiting for transfers between devices: none -> 70.9 us  [_perform_spots(): lax.all_to_all(jnp.stack(lax.axis_size(bus_axis) * [u_in]), bus_axis, 0, 0)]
where the time goes in v1:
time: 1330 us; the launch traced here: 1320 us
  waiting for transfers between devices  816 us (61%)
  other arithmetic  339 us (25%)
  matrix products  57.5 us (4%)
  local copies, waits for them, and re-layouts  50 us (4%)
  blocking collectives  34.8 us (3%)
  between operations  20.9 us (2%)
    psum x5, waiting for transfers between devices, from_root(): return lax.psum(jnp.where(mine, value, jnp.zeros_like(value)), axis)  745 us
    another operation x19, other arithmetic, per_device(): jnp.linalg.cholesky(jnp.where(samp_index == 1, update, identity))  108 us
    another operation x18, other arithmetic, per_device(): jnp.linalg.cholesky(jnp.where(samp_index == 0, first_cols, identity))  107 us
    another operation x5, other arithmetic, right_solve(): return jax.scipy.linalg.solve_triangular(factor, block.T, lower=True).T  104 us
    all_to_all x1, waiting for transfers between devices, _perform_spots(): lax.all_to_all(jnp.stack(lax.axis_size(bus_axis) * [u_in]), bus_axis, 0, 0)  70.9 us
    psum x1, blocking collectives, per_device(): moment_one, moment_two = lax.psum((sum_one, sum_two), 'samp')  34.8 us
    another operation x41, local copies, waits for them, and re-layouts, right_solve(): return jax.scipy.linalg.solve_triangular(factor, block.T, lower=True).T  29.1 us
  transfers between devices with their start and end apart: 6, of which 6 were waited for; matrix products, arithmetic and copies ran while one was open for 0% of the time, Pallas kernels for 0%

profile of v1, /device:TPU:1, one launch (start us, length us, event | category | flops | bytes accessed | tf_op | source)
XLA Modules:
  0.0 1324.2 jit_solution(14180577896767023048)
XLA Ops:
  10.4 34.8 %all-reduce.1 = (f32[2,256]{1,0:T(2,128)S(1)}, f32[2,256]{1,0:T(2,128)S(1)}) all-reduce(f32[2,256]{1,0:T(2,128)S(1)} %fusion.8, f32[2,256]{1,0:T(2,128)S(1)} %fusion.104), channel_id=1, replica_groups=mesh['samp'=16,'par'=8] {'samp'}, use_global_device_ids=true, to_apply=%region_2.0 | all-reduce | flops 1024 | bytes 8192 | tf_op jit(solution)/shard_map/psum | solution.py:61
  45.5 3.0 stack.2
  48.4 4.7 all-to-all-start
  53.2 70.9 %all-to-all-done = bf16[8,640,2,256]{1,3,2,0:T(8,128)(2,1)} async-done(((bf16[8,640,2,256]{1,3,2,0:T(8,128)(2,1)}), bf16[8,640,2,256]{1,3,2,0:T(8,128)(2,1)}, u32[]{:S(2)}, u32[]{:S(2)}) %all-to-all-start) | async-done | bytes 5242912 | tf_op jit(solution)/shard_map/all_to_all | solution.py:13
  124.1 2.9 copy.43
  127.1 5.6 broadcast_select_fusion.1
  133.1 168.3 %all-reduce.17.cloned.1.call-done = (bf16[640,4096]{0,1:T(8,128)(2,1)}, bf16[640,4096]{0,1:T(8,128)(2,1)}) async-done(((bf16[640,4096]{0,1:T(8,128)(2,1)}, bf16[640,4096]{0,1:T(8,128)(2,1)}), (bf16[640,4096]{0,1:T(8,128)(2,1)}, bf16[640,4096]{0,1:T(8,128)(2,1)})) %all-reduce.17.cloned.1.call-update) | async-done | bytes 10485776 | tf_op jit(solution)/shard_map/psum | solution.py:22
  301.4 8.6 fusion.105
  310.1 4.5 fusion.106
  314.6 3.3 broadcast_select_fusion.2
  318.0 149.1 %all-reduce.9.cloned.1.call-done = f32[640,1280]{0,1:T(8,128)} async-done(((f32[640,1280]{0,1:T(8,128)}), f32[640,1280]{0,1:T(8,128)}) %all-reduce.9.cloned.1.call-update) | async-done | bytes 3276816 | tf_op jit(solution)/shard_map/psum | solution.py:22
  467.1 2.8 convert_select_fusion.1
  469.9 1.6 copy.44
  472.9 11.7 cholesky.364
  484.7 9.8 custom-call.34
  495.9 13.2 cholesky.383
  509.1 1.5 select_reduce_fusion.8
  510.6 11.4 custom-call.35
  523.6 12.3 cholesky.404
  537.5 10.4 custom-call.36
  549.6 11.9 cholesky.423
  562.2 9.8 custom-call.37
  572.6 11.7 cholesky.440
  590.2 144.2 %all-reduce.11.cloned.1.call-done = f32[640,640]{1,0:T(8,128)} async-done(((f32[640,640]{1,0:T(8,128)}), f32[640,640]{1,0:T(8,128)}) %all-reduce.11.cloned.1.call-update) | async-done | bytes 1638416 | tf_op jit(solution)/shard_map/psum | solution.py:22
  734.4 2.7 fusion.4
  737.2 14.3 %while.4 = (s32[]{:T(128)}, f32[640,640]{1,0:T(8,128)}, s32[5,2]{0,1:T(2,128)S(1)}, f32[5,128,128]{2,1,0:T(8,128)S(1)}, s32[]{:T(128)}) while((s32[]{:T(128)}, f32[640,640]{1,0:T(8,128)}, s32[5,2]{0,1:T(2,128)S(1)}, f32[5,128,128]{2,1,0:T(8,128)S(1)}, s32[]{:T(128)}) %tuple.67), condition=%wide.while_cond, body=%wide.while_body.sunk | while | flops 2 | bytes 131181 | solution.py:26
  738.2 2.2 bitcast_dynamic-update-slice_fusion.4
  741.0 2.2 bitcast_dynamic-update-slice_fusion.4
  743.8 2.2 bitcast_dynamic-update-slice_fusion.4
  746.6 2.2 bitcast_dynamic-update-slice_fusion.4
  749.4 2.1 bitcast_dynamic-update-slice_fusion.4
  751.5 49.1 %custom-call.38 = f32[5,128,128]{1,2,0:T(8,128)S(1)} custom-call(f32[5,128,128]{2,1,0:T(8,128)S(1)} %get-tuple-element.18), custom_call_target="InvertDiagBlocksLowerTriangular" | custom-call | tf_op jit(solution)/shard_map/jit(_solve_triangular)/triangular_solve | solution.py:26
  804.8 1.8 convolution_subtract_fusion.5
  807.1 1.9 fusion.28
  809.8 1.5 convolution_dynamic-update-slice_fusion.1
  812.7 144.2 %all-reduce.13.cloned.1.call-done = f32[640,640]{1,0:T(8,128)} async-done(((f32[640,640]{1,0:T(8,128)}), f32[640,640]{1,0:T(8,128)}) %all-reduce.13.cloned.1.call-update) | async-done | bytes 1638416 | tf_op jit(solution)/shard_map/psum | solution.py:22
  956.8 7.7 convert_select_fusion
  964.5 1.8 copy.53
  966.3 1.6 fusion
  969.1 11.7 cholesky.455
  981.0 9.8 custom-call.39
  994.1 13.2 cholesky.474
  1007.2 1.5 select_reduce_fusion.3
  1010.1 11.5 custom-call.40
  1024.1 12.3 cholesky.495
  1038.0 10.4 custom-call.41
  1050.9 12.1 cholesky.514
  1063.7 9.8 custom-call.42
  1074.9 11.7 cholesky.531
  1091.8 4.6 copy.60
  1096.4 139.5 %all-reduce.15.cloned.1.call-done = f32[640,640]{1,0:T(8,128)} async-done(((f32[640,640]{1,0:T(8,128)}), f32[640,640]{1,0:T(8,128)}) %all-reduce.15.cloned.1.call-update) | async-done | bytes 1638416 | tf_op jit(solution)/shard_map/psum | solution.py:22
  1235.9 1.5 fusion.2
  1238.2 13.2 while.5
  1238.8 2.0 bitcast_dynamic-update-slice_fusion.5
  1241.5 2.0 bitcast_dynamic-update-slice_fusion.5
  1244.1 2.0 bitcast_dynamic-update-slice_fusion.5
  1246.8 2.0 bitcast_dynamic-update-slice_fusion.5
  1249.4 2.0 bitcast_dynamic-update-slice_fusion.5
  1251.4 50.8 %custom-call.43 = f32[5,128,128]{1,2,0:T(8,128)} custom-call(f32[5,128,128]{2,1,0:T(8,128)} %get-tuple-element.19), custom_call_target="InvertDiagBlocksLowerTriangular" | custom-call | tf_op jit(solution)/shard_map/jit(_solve_triangular)/triangular_solve | solution.py:26
  1302.2 1.5 fusion.52
  1305.6 1.6 convolution_subtract_fusion
  1307.7 2.0 convolution_subtract_fusion.4
  1310.1 2.7 fusion.25
  1314.5 1.5 convolution_dynamic-update-slice_fusion
  (143 shorter events, 52.0 us)
Async XLA Ops:
  48.4 75.7 %all-to-all-start = ((bf16[8,640,2,256]{1,3,2,0:T(8,128)(2,1)}), bf16[8,640,2,256]{1,3,2,0:T(8,128)(2,1)}, u32[]{:S(2)}, u32[]{:S(2)}) async-start(bf16[8,640,2,256]{1,3,2,0:T(8,128)(2,1)} %stack.2), calls=%async_computation | async-start | bytes 10485760 | tf_op jit(solution)/shard_map/all_to_all | solution.py:13
  53.1 248.3 %all-reduce.17.cloned.1.call-start = ((), (), s32[]{:S(2)}) async-start(), calls=%async_computation.5 | async-start | bytes 20971520 | tf_op jit(solution)/shard_map/psum | solution.py:22
  127.1 5.6 copy-start
  132.7 177.4 %slice-start = ((s8[5242880]{0:T(1024)(128)(4,1)}), s8[1048576]{0:T(1024)(128)(4,1)S(1)}, s32[]{:S(2)}) async-start(s8[5242880]{0:T(1024)(128)(4,1)} %bitcast.135), calls=%async_computation.6 | async-start | bytes 2097152
  132.7 334.4 %all-reduce.9.cloned.1.call-start = ((), (), s32[]{:S(2)}) async-start(), calls=%async_computation.1 | async-start | bytes 6553600 | tf_op jit(solution)/shard_map/psum | solution.py:22
  301.4 8.6 slice-start.1
  301.4 8.7 copy-start.9
  317.9 416.5 %all-reduce.11.cloned.1.call-start = ((), (), s32[]{:S(2)}) async-start(), calls=%async_computation.2 | async-start | bytes 3276800 | tf_op jit(solution)/shard_map/psum | solution.py:22
  471.7 1.2 copy-start.3
  472.9 21.7 %copy-start.4 = (f32[640,640]{1,0:T(8,128)S(1)}, f32[640,640]{1,0:T(8,128)}, u32[]{:S(2)}) copy-start(f32[640,640]{1,0:T(8,128)} %copy-done.3) | copy-start | bytes 4915204
  590.1 366.7 %all-reduce.13.cloned.1.call-start = ((), (), s32[]{:S(2)}) async-start(), calls=%async_computation.3 | async-start | bytes 3276800 | tf_op jit(solution)/shard_map/psum | solution.py:22
  590.2 210.5 %copy-start.1 = (f32[640,640]{1,0:T(8,128)S(1)}, f32[640,640]{1,0:T(8,128)}, u32[]{:S(2)}) copy-start(f32[640,640]{1,0:T(8,128)} %get-tuple-element.55) | copy-start | bytes 4915204
  800.6 6.0 copy-start.7
  812.6 423.3 %all-reduce.15.cloned.1.call-start = ((), (), s32[]{:S(2)}) async-start(), calls=%async_computation.4 | async-start | bytes 3276800 | tf_op jit(solution)/shard_map/psum | solution.py:22
  967.9 1.2 copy-start.2
  1251.4 50.8 %copy-start.5 = (f32[640,640]{1,0:T(8,128)}, f32[640,640]{1,0:T(8,128)S(1)}, u32[]{:S(2)}) copy-start(f32[640,640]{1,0:T(8,128)S(1)} %get-tuple-element.201) | copy-start | bytes 4915204
  1302.2 3.0 copy-start.8
  1313.5 1.0 copy-start.6
Sparse Core Ops, SparseCore 0:
  132.8 168.5 all-reduce.16
  318.1 149.0 all-reduce.8
  590.2 144.1 all-reduce.10
  812.7 144.0 all-reduce.12
  1091.9 143.8 all-reduce.14
